TPU v7x, 512 devices: a whole 4x4x16 slice. The times are simulated.
512 devices in a mesh: leaf: 128 (over z, y, core), rep: 4 (over x).
Axes of the slice: x: 4, y: 4, z: 16, core: 2. Of those that a mesh axis runs over, the one named last changes fastest.
Arguments:
- positions: float32 [3, 8192, 128], P(None, ('leaf', 'rep')), may hold values from -6 to 6
- density: float32 [3, 8192, 128], P(None, ('leaf', 'rep')), may hold values from -6 to 6
- near_offset: int32 [8192, 12], P(('leaf', 'rep')), may hold values from -2 to 2
- near_count: int32 [8192], P(('leaf', 'rep')), may hold values from 1 to 12
- inter_list: int32 [512, 189], P(('leaf', 'rep')), may hold values from 0 to 511
- operator_index: int32 [512, 189], P(('leaf', 'rep')), may hold values from 0 to 3
- lattice_index: int32 [512], P(('leaf', 'rep')), may hold values from 0 to 1
- up_weight: bfloat16 [512, 384], replicated, may hold values from -0.3125 to 0.3125
- m2l_operators: bfloat16 [4, 512, 512], replicated, may hold values from -0.0390625 to 0.0390625
- lattice_operators: bfloat16 [2, 512, 512], replicated, may hold values from -0.01171875 to 0.01171875
- down_weight: bfloat16 [384, 512], replicated, may hold values from -0.5 to 0.5
Outputs:
- velocity: float32 [3, 8192, 128], P(None, ('leaf', 'rep'))
Inputs may be any that keep to these rules, and one draw needn't show every extreme that they name: `near_offset`: leaf g's near source leaves are (g + offset) mod 8192; slots at or past near_count are unused.
All inputs are finite; a program needn't handle non-finite values.
Results may differ from a plain program's by a relative error of at most 0.02.
Values may be sent and summed in bfloat16 or wider, within the bound.
A program may use at most 64 MiB of HBM per device.

v0:
```python
import math
import jax
import jax.numpy as jnp
from jax import lax
from jax.sharding import PartitionSpec as P


def padded(shard, sides, width):
    for axis, dim in sides:
        size, length = (lax.axis_size(axis), shard.shape[dim])
        up = [(i, (i + 1) % size) for i in range(size)]
        down = [(j, i) for i, j in up]
        last = lax.slice_in_dim(shard, length - width, length, axis=dim)
        first = lax.slice_in_dim(shard, 0, width, axis=dim)
        before = lax.ppermute(last, axis, up)
        after = lax.ppermute(first, axis, down)
        shard = jnp.concatenate([before, shard, after], axis=dim)
    return shard


def stokes_tile(target, source_pos, source_force, live_slots):
    offsets_xyz = target[:, None, :, None] - source_pos[:, :, None, :]
    distance_sq = jnp.sum(offsets_xyz * offsets_xyz, axis=0) + 0.05
    inverse = lax.rsqrt(distance_sq)
    inverse_cube = inverse * inverse * inverse
    projected = jnp.sum(offsets_xyz * source_force[:, :, None, :], axis=0)
    kernel_terms = source_force[:, :, None, :] * inverse + offsets_xyz * (projected * inverse_cube)
    kernel_terms = kernel_terms * live_slots[None, :, None, None]
    return jnp.sum(kernel_terms, axis=(1, 3)) * (1.0 / (8.0 * math.pi))


def body(
    positions,
    density,
    near_offset,
    near_count,
    inter_list,
    operator_index,
    lattice_index,
    up_weight,
    m2l_operators,
    lattice_operators,
    down_weight,
):
    per_box = positions.shape[1]
    node_count = positions.shape[2]
    kind_count = m2l_operators.shape[0]
    stacked = jnp.concatenate([positions, density], axis=0)
    extended = padded(stacked.astype(jnp.bfloat16), ((("leaf", "rep"), 1),), per_box).astype(
        stacked.dtype
    )
    slot_range = jnp.arange(near_offset.shape[1], dtype=jnp.int32)

    def one_leaf(leaf_slot):
        target = positions[:, leaf_slot]
        source_slot = leaf_slot + near_offset[leaf_slot] + per_box
        sources = jnp.take(extended, source_slot, axis=1)
        live_slots = (slot_range < near_count[leaf_slot]).astype(jnp.float32)
        return stokes_tile(target, sources[:3], sources[3:], live_slots)

    near_part = lax.map(one_leaf, jnp.arange(per_box, dtype=jnp.int32))
    near_part = jnp.transpose(near_part, (1, 0, 2))
    damping = 1.0 / (1.0 + jnp.sum(positions * positions, axis=0))
    summed = jnp.sum(density * damping[None], axis=1).reshape(-1).astype(jnp.bfloat16)
    coarse = jnp.dot(up_weight, summed, preferred_element_type=jnp.float32).astype(jnp.bfloat16)
    coarse_row = coarse.reshape(1, -1)
    box_ids = inter_list[0]
    op_kinds = operator_index[0]
    kind_range = jnp.arange(kind_count, dtype=jnp.int32)
    selector = (op_kinds[None, :] == kind_range[:, None]).astype(jnp.float32)
    all_blocks = lax.all_gather(coarse_row, ("leaf", "rep"), axis=0, tiled=True)
    chosen = jnp.take(all_blocks, box_ids, axis=0).astype(jnp.float32)
    grouped_sum = jnp.dot(selector, chosen, precision=lax.Precision.HIGHEST)
    block_sum = jnp.sum(all_blocks.astype(jnp.float32), axis=0)
    block_sum = lax.psum(coarse.astype(jnp.float32), ("leaf", "rep"))
    total = block_sum.astype(jnp.bfloat16)
    grouped = grouped_sum.astype(jnp.bfloat16)
    local = jnp.einsum("tij,tj->i", m2l_operators, grouped, preferred_element_type=jnp.float32)
    local = local + jnp.dot(
        lattice_operators[lattice_index[0]], total, preferred_element_type=jnp.float32
    )
    local_bf = local.astype(jnp.bfloat16)
    far_part = jnp.dot(down_weight, local_bf, preferred_element_type=jnp.float32).reshape(
        3, node_count
    )
    return near_part + damping[None] * far_part[:, None, :]


def solution(mesh):
    in_specs = (
        P(None, ("leaf", "rep"), None),
        P(None, ("leaf", "rep"), None),
        P(("leaf", "rep"), None),
        P(("leaf", "rep")),
        P(("leaf", "rep"), None),
        P(("leaf", "rep"), None),
        P(("leaf", "rep")),
        P(),
        P(),
        P(),
        P(),
    )
    out_specs = P(None, ("leaf", "rep"), None)
    return jax.shard_map(body, mesh=mesh, in_specs=in_specs, out_specs=out_specs, check_vma=False)
```

profile of v0, /device:TPU:4, one launch (start us, length us, event | category | flops | bytes accessed | tf_op | source)
XLA Modules:
  0.0 417.0 jit_solution(9846070013614672958)
XLA Ops:
  0.0 0.9 multiply_reduce_fusion.1
  0.9 0.8 multiply_reduce_fusion
  1.8 3.1 collective-permute-start
  4.9 2.7 collective-permute-start.1
  7.7 1.2 fusion.22
  8.9 108.3 %psum.7 = bf16[512]{0:T(512)(128)(2,1)S(1)} all-reduce(bf16[512]{0:T(512)(128)(2,1)S(1)} %convert_element_type.40), channel_id=1, replica_groups=mesh['leaf'=128,'rep'=4] {'leaf','rep'}, use_global_device_ids=true, to_apply=%region_7.8 | all-reduce | flops 512 | bytes 2048 | tf_op jit(solution)/shard_map/psum | solution.py:75
  117.8 136.1 %all-gather.1 = bf16[512,1,512]{2,1,0:T(2,128)(2,1)S(1)} all-gather(bf16[1,1,512]{2,1,0:T(2,128)(2,1)S(1)} %reshape.142), channel_id=2, replica_groups=mesh['leaf'=128,'rep'=4] {'leaf','rep'}, dimensions={0}, use_global_device_ids=true | all-gather | bytes 525312 | tf_op jit(solution)/shard_map/all_gather | solution.py:71
  254.2 1.0 gather_fusion.1
  256.0 1.3 fusion.10
  257.8 158.6 %while.13 = (s32[]{:T(128)}, f32[16,3,128]{2,0,1:T(8,128)S(1)}, s32[16]{0:T(128)S(1)}, s32[16,12]{1,0:T(8,128)}, f32[6,48,128]{2,0,1:T(8,128)S(1)}, /*index=5*/f...) while((s32[]{:T(128)}, f32[16,3,128]{2,0,1:T(8,128)S(1)}, ...), condition=%wide.region_4.5_spmd.clone, body=%wide.region_0.4_spmd.clone.sunk | while | flops 6891705 | bytes 6684707 | solution.py:61
  260.5 1.4 fusion.33
  262.5 1.4 compare_and_fusion.3
  264.0 0.7 constant_dynamic-slice_fusion.2
  270.4 1.4 fusion.33
  272.4 1.4 compare_and_fusion.3
  273.9 0.7 constant_dynamic-slice_fusion.2
  280.3 1.4 fusion.33
  282.3 1.4 compare_and_fusion.3
  290.3 1.4 fusion.33
  292.2 1.4 compare_and_fusion.3
  293.7 0.7 constant_dynamic-slice_fusion.2
  300.2 1.4 fusion.33
  302.1 1.4 compare_and_fusion.3
  310.1 1.4 fusion.33
  312.0 1.4 compare_and_fusion.3
  313.6 0.7 constant_dynamic-slice_fusion.2
  320.0 1.4 fusion.33
  322.0 1.4 compare_and_fusion.3
  323.5 0.7 constant_dynamic-slice_fusion.2
  329.9 1.4 fusion.33
  331.9 1.4 compare_and_fusion.3
  333.4 0.7 constant_dynamic-slice_fusion.2
  339.8 1.4 fusion.33
  341.8 1.4 compare_and_fusion.3
  349.7 1.4 fusion.33
  351.7 1.4 compare_and_fusion.3
  359.6 1.4 fusion.33
  361.6 1.4 compare_and_fusion.3
  369.6 1.4 fusion.33
  371.5 1.4 compare_and_fusion.3
  379.5 1.4 fusion.33
  381.4 1.4 compare_and_fusion.3
  389.4 1.4 fusion.33
  391.3 1.4 compare_and_fusion.3
  399.3 1.4 fusion.33
  401.3 1.4 compare_and_fusion.3
  409.2 1.4 fusion.33
  411.2 1.4 compare_and_fusion.3
  (298 shorter events, 77.1 us)
Async XLA Ops:
  0.0 255.4 %copy-start = (bf16[4,512,512]{2,1,0:T(8,128)(2,1)S(1)}, bf16[4,512,512]{2,1,0:T(8,128)(2,1)}, u32[]{:S(2)}) copy-start(bf16[4,512,512]{2,1,0:T(8,128)(2,1)} %param.21) | copy-start | bytes 6291460
  0.0 254.1 %copy-start.2 = (s32[1,189]{1,0:T(1,128)S(1)}, s32[1,189]{1,0:T(1,128)}, u32[]{:S(2)}) copy-start(s32[1,189]{1,0:T(1,128)} %param.17) | copy-start | bytes 2272
  1.8 255.9 %collective-permute-start = (bf16[6,16,128]{2,1,0:T(8,128)(2,1)S(1)}, bf16[6,16,128]{2,1,0:T(8,128)(2,1)S(1)}, u32[]{:S(2)}, u32[]{:S(2)}) collective-permute-start(bf16[6,16,128]{2,1,0:T(8,128)(2,1)S(1)} %pad_maximum_fusion), channel_id=1, source_target_pairs={{0,1},{1,2},{2,3},{3,4},{4,5},{5,6},{6,7},{7,8},{8,9},{9,10},{10,1... | collective-permute-start | bytes 73736 | tf_op jit(solution)/shard_map/ppermute | solution.py:15
  4.9 252.8 %collective-permute-start.1 = (bf16[6,16,128]{2,1,0:T(8,128)(2,1)S(1)}, bf16[6,16,128]{2,1,0:T(8,128)(2,1)S(1)}, u32[]{:S(2)}, u32[]{:S(2)}) collective-permute-start(bf16[6,16,128]{2,1,0:T(8,128)(2,1)S(1)} %pad_maximum_fusion), channel_id=1, source_target_pairs={{1,0},{2,1},{3,2},{4,3},{5,4},{6,5},{7,6},{8,7},{9,8},{10,9},{11,1... | collective-permute-start | bytes 73736 | tf_op jit(solution)/shard_map/ppermute | solution.py:16
  117.8 137.4 %copy-start.3 = (s32[1,189]{1,0:T(1,128)S(1)}, s32[1,189]{1,0:T(1,128)}, u32[]{:S(2)}) copy-start(s32[1,189]{1,0:T(1,128)} %param.18) | copy-start | bytes 2272
  254.1 3.2 copy-start.1
  255.2 2.6 copy-start.4
where the time goes:
time: 420 us; the launch traced here: 417 us
  blocking collectives  244 us (58%)
  other arithmetic  83.3 us (20%)
  local copies, waits for them, and re-layouts  44.2 us (11%)
  loops' own time  34.7 us (8%)
  starting transfers between devices  5.84 us (1%)
    all_gather x1, blocking collectives, body(): all_blocks = lax.all_gather(coarse_row, ('leaf', 'rep'), axis=0, tiled=True)  136 us
    psum x1, blocking collectives, body(): block_sum = lax.psum(coarse.astype(jnp.float32), ('leaf', 'rep'))  108 us
    another operation x1, loops' own time, body(): near_part = lax.map(one_leaf, jnp.arange(per_box, dtype=jnp.int32))  34.7 us
    select_n x32, other arithmetic, one_leaf(): sources = jnp.take(extended, source_slot, axis=1)  23.5 us
    and x16, other arithmetic, one_leaf(): sources = jnp.take(extended, source_slot, axis=1)  22.2 us
    dynamic_slice x32, local copies, waits for them, and re-layouts, one_leaf(): target = positions[:, leaf_slot]  11.6 us
    convert_element_type x16, other arithmetic, one_leaf(): live_slots = (slot_range < near_count[leaf_slot]).astype(jnp.float32)  11 us
    reduce_sum x16, other arithmetic, stokes_tile(): return jnp.sum(kernel_terms, axis=(1, 3)) * (1.0 / (8.0 * math.pi))  10.7 us
  transfers between devices with their start and end apart: 2, of which 0 were waited for; matrix products, arithmetic and copies ran while one was open for 1% of the time, Pallas kernels for 0%

commit v1 on v0

--- a/solution.py
+++ b/solution.py
@@ -3,6 +3,12 @@
 import jax.numpy as jnp
 from jax import lax
 from jax.sharding import PartitionSpec as P
+
+
+def add_all(shard, mesh_axis):
+    shards = lax.all_gather(shard, mesh_axis, axis=0, tiled=False)
+    total = shards.sum(axis=0)
+    return total
 
 
 def padded(shard, sides, width):
@@ -72,7 +78,7 @@
     chosen = jnp.take(all_blocks, box_ids, axis=0).astype(jnp.float32)
     grouped_sum = jnp.dot(selector, chosen, precision=lax.Precision.HIGHEST)
     block_sum = jnp.sum(all_blocks.astype(jnp.float32), axis=0)
-    block_sum = lax.psum(coarse.astype(jnp.float32), ("leaf", "rep"))
+    block_sum = add_all(coarse.astype(jnp.float32), ("leaf", "rep"))
     total = block_sum.astype(jnp.bfloat16)
     grouped = grouped_sum.astype(jnp.bfloat16)
     local = jnp.einsum("tij,tj->i", m2l_operators, grouped, preferred_element_type=jnp.float32)

time: 420 us -> 322 us (0.77)
  the two profiles are of different devices: /device:TPU:4 before, /device:TPU:2 now
where the time goes in v1:
time: 322 us; the launch traced here: 319 us
  blocking collectives  142 us (44%)
  other arithmetic  79.5 us (25%)
  local copies, waits for them, and re-layouts  41.7 us (13%)
  loops' own time  28.5 us (9%)
  between operations  14.3 us (4%)
  starting transfers between devices  9.74 us (3%)
  matrix products  3.57 us (1%)
    all_gather x1, blocking collectives, body(): all_blocks = lax.all_gather(coarse_row, ('leaf', 'rep'), axis=0, tiled=True)  142 us
    another operation x1, loops' own time, body(): near_part = lax.map(one_leaf, jnp.arange(per_box, dtype=jnp.int32))  28.5 us
    select_n x32, other arithmetic, one_leaf(): sources = jnp.take(extended, source_slot, axis=1)  21.4 us
    and x16, other arithmetic, one_leaf(): sources = jnp.take(extended, source_slot, axis=1)  20.2 us
    dynamic_slice x32, local copies, waits for them, and re-layouts, one_leaf(): target = positions[:, leaf_slot]  11.6 us
    reduce_sum x16, other arithmetic, stokes_tile(): return jnp.sum(kernel_terms, axis=(1, 3)) * (1.0 / (8.0 * math.pi))  10.7 us
    reduce_sum x16, other arithmetic, stokes_tile(): distance_sq = jnp.sum(offsets_xyz * offsets_xyz, axis=0) + 0.05  10.2 us
    dynamic_slice x16, local copies, waits for them, and re-layouts, one_leaf(): live_slots = (slot_range < near_count[leaf_slot]).astype(jnp.float32)  9.42 us
  transfers between devices with their start and end apart: 3, of which 0 were waited for; matrix products, arithmetic and copies ran while one was open for 37% of the time, Pallas kernels for 0%

profile of v1, /device:TPU:2, one launch (start us, length us, event | category | flops | bytes accessed | tf_op | source)
XLA Modules:
  0.0 319.1 jit_solution(14168430391813079792)
XLA Ops:
  6.5 0.9 multiply_reduce_fusion.1
  7.5 0.8 multiply_reduce_fusion
  8.3 3.4 %collective-permute-start = (bf16[6,16,128]{2,1,0:T(8,128)(2,1)S(1)}, bf16[6,16,128]{2,1,0:T(8,128)(2,1)S(1)}, u32[]{:S(2)}, u32[]{:S(2)}) collective-permute-start(bf16[6,16,128]{2,1,0:T(8,128)(2,1)S(1)} %pad_maximum_fusion), channel_id=1, source_target_pairs={{0,1},{1,2},{2,3},{3,4},{4,5},{5,6},{6,7},{7,8},{8,9},{9,10},{10,1... | collective-permute-start | bytes 73736 | tf_op jit(solution)/shard_map/ppermute | solution.py:21
  11.7 6.3 %collective-permute-start.1 = (bf16[6,16,128]{2,1,0:T(8,128)(2,1)S(1)}, bf16[6,16,128]{2,1,0:T(8,128)(2,1)S(1)}, u32[]{:S(2)}, u32[]{:S(2)}) collective-permute-start(bf16[6,16,128]{2,1,0:T(8,128)(2,1)S(1)} %pad_maximum_fusion), channel_id=1, source_target_pairs={{1,0},{2,1},{3,2},{4,3},{5,4},{6,5},{7,6},{8,7},{9,8},{10,9},{11,1... | collective-permute-start | bytes 73736 | tf_op jit(solution)/shard_map/ppermute | solution.py:22
  18.1 1.2 fusion.23
  19.9 141.8 %all-gather.2 = bf16[512,1,512]{2,1,0:T(2,128)(2,1)S(1)} all-gather(bf16[1,1,512]{2,1,0:T(2,128)(2,1)S(1)} %reshape.144), channel_id=2, replica_groups=mesh['leaf'=128,'rep'=4] {'leaf','rep'}, dimensions={0}, use_global_device_ids=true | all-gather | bytes 525312 | tf_op jit(solution)/shard_map/all_gather | solution.py:77
  161.9 1.0 gather_fusion.1
  164.6 143.5 %while.13 = (s32[]{:T(128)}, f32[16,3,128]{2,0,1:T(8,128)S(1)}, s32[16]{0:T(128)S(1)}, s32[16,12]{1,0:T(8,128)}, f32[6,48,128]{2,0,1:T(8,128)S(1)}, /*index=5*/f...) while((s32[]{:T(128)}, f32[16,3,128]{2,0,1:T(8,128)S(1)}, ...), condition=%wide.region_4.5_spmd.clone, body=%wide.region_0.4_spmd.clone.sunk | while | flops 6891705 | bytes 6684707 | solution.py:67
  166.9 1.3 fusion.34
  168.7 1.3 compare_and_fusion.3
  170.1 0.7 constant_dynamic-slice_fusion.2
  175.9 1.3 fusion.34
  177.7 1.3 compare_and_fusion.3
  184.8 1.3 fusion.34
  186.7 1.3 compare_and_fusion.3
  188.1 0.7 constant_dynamic-slice_fusion.2
  193.8 1.3 fusion.34
  195.6 1.3 compare_and_fusion.3
  197.0 0.7 constant_dynamic-slice_fusion.2
  202.8 1.3 fusion.34
  204.6 1.3 compare_and_fusion.3
  211.8 1.3 fusion.34
  213.6 1.3 compare_and_fusion.3
  215.0 0.7 constant_dynamic-slice_fusion.2
  220.7 1.3 fusion.34
  222.6 1.3 compare_and_fusion.3
  223.9 0.7 constant_dynamic-slice_fusion.2
  229.7 1.3 fusion.34
  231.5 1.3 compare_and_fusion.3
  238.7 1.3 fusion.34
  240.5 1.3 compare_and_fusion.3
  241.9 0.7 constant_dynamic-slice_fusion.2
  247.6 1.3 fusion.34
  249.5 1.3 compare_and_fusion.3
  256.6 1.3 fusion.34
  258.4 1.3 compare_and_fusion.3
  265.6 1.3 fusion.34
  267.4 1.3 compare_and_fusion.3
  274.5 1.3 fusion.34
  276.4 1.3 compare_and_fusion.3
  283.5 1.3 fusion.34
  285.3 1.3 compare_and_fusion.3
  292.5 1.3 fusion.34
  294.3 1.3 compare_and_fusion.3
  301.5 1.3 fusion.34
  303.3 1.3 compare_and_fusion.3
  308.2 1.8 reduce_sum.65
  310.0 1.3 fusion.10
  (301 shorter events, 73.1 us)
Async XLA Ops:
  6.5 156.6 %copy-start = (bf16[4,512,512]{2,1,0:T(8,128)(2,1)S(1)}, bf16[4,512,512]{2,1,0:T(8,128)(2,1)}, u32[]{:S(2)}) copy-start(bf16[4,512,512]{2,1,0:T(8,128)(2,1)} %param.21) | copy-start | bytes 6291460
  6.5 155.4 %copy-start.2 = (s32[1,189]{1,0:T(1,128)S(1)}, s32[1,189]{1,0:T(1,128)}, u32[]{:S(2)}) copy-start(s32[1,189]{1,0:T(1,128)} %param.17) | copy-start | bytes 2272
  6.5 301.6 %all-gather.6.cloned.1.call-start = ((), (), s32[]{:S(2)}) async-start(), calls=%async_computation | async-start | bytes 1050624 | tf_op jit(solution)/shard_map/all_gather | solution.py:9
  8.3 156.2 %collective-permute-start = (bf16[6,16,128]{2,1,0:T(8,128)(2,1)S(1)}, bf16[6,16,128]{2,1,0:T(8,128)(2,1)S(1)}, u32[]{:S(2)}, u32[]{:S(2)}) collective-permute-start(bf16[6,16,128]{2,1,0:T(8,128)(2,1)S(1)} %pad_maximum_fusion), channel_id=1, source_target_pairs={{0,1},{1,2},{2,3},{3,4},{4,5},{5,6},{6,7},{7,8},{8,9},{9,10},{10,1... | collective-permute-start | bytes 73736 | tf_op jit(solution)/shard_map/ppermute | solution.py:21
  11.7 152.8 %collective-permute-start.1 = (bf16[6,16,128]{2,1,0:T(8,128)(2,1)S(1)}, bf16[6,16,128]{2,1,0:T(8,128)(2,1)S(1)}, u32[]{:S(2)}, u32[]{:S(2)}) collective-permute-start(bf16[6,16,128]{2,1,0:T(8,128)(2,1)S(1)} %pad_maximum_fusion), channel_id=1, source_target_pairs={{1,0},{2,1},{3,2},{4,3},{5,4},{6,5},{7,6},{8,7},{9,8},{10,9},{11,1... | collective-permute-start | bytes 73736 | tf_op jit(solution)/shard_map/ppermute | solution.py:22
  19.9 143.0 %copy-start.3 = (s32[1,189]{1,0:T(1,128)S(1)}, s32[1,189]{1,0:T(1,128)}, u32[]{:S(2)}) copy-start(s32[1,189]{1,0:T(1,128)} %param.18) | copy-start | bytes 2272
  161.9 2.7 copy-start.4
  164.6 146.7 %copy-start.1 = (bf16[384,512]{1,0:T(8,128)(2,1)S(1)}, bf16[384,512]{1,0:T(8,128)(2,1)}, u32[]{:S(2)}) copy-start(bf16[384,512]{1,0:T(8,128)(2,1)} %param.23) | copy-start | bytes 1179652
Sparse Core Ops, SparseCore 0:
  20.0 168.4 all-gather.5
